TPU v7x, 256 devices: a whole 4x4x8 slice. The times are simulated.
256 devices in a mesh: seq: 32 (over x, y, core), head: 8 (over z).
Axes of the slice: x: 4, y: 4, z: 8, core: 2. Of those that a mesh axis runs over, the one named last changes fastest.
Arguments:
- query_rows: bfloat16 [4096, 3072], P('seq', 'head'), may hold values from -30 to 30
- key_rows: bfloat16 [4096, 3072], P('seq', 'head'), may hold values from -22.5 to 22.5
- value_rows: bfloat16 [4096, 3072], P('seq', 'head'), may hold values from -6 to 6
- output_grad: bfloat16 [4096, 5120], P('seq', 'head'), may hold values from -6 to 6
- out_weight: bfloat16 [5120, 3072], P(None, 'head'), may hold values from -0.078125 to 0.078125
- clusters: int32 [64], replicated, may hold values from 0 to 3
Outputs:
- query_grad: bfloat16 [4096, 3072], P('seq', 'head')
- key_grad: bfloat16 [4096, 3072], P('seq', 'head')
- value_grad: bfloat16 [4096, 3072], P('seq', 'head')
Inputs may be any that keep to these rules, and one draw needn't show every extreme that they name: `clusters`: cluster of each block of 64 tokens.
All inputs are finite; a program needn't handle non-finite values.
Results may differ from a plain program's by a relative error of at most 0.023.
Values may be sent and summed in bfloat16 or wider, within the bound.
No kernel may reach another device: no remote copies, remote signals or barrier semaphores. Data moves between devices by JAX's collectives and lax.ppermute only.
A program may use at most 64 MiB of HBM per device.

v0:
```python
import jax
import jax.numpy as jnp
from jax import lax
from jax.sharding import PartitionSpec as P

HS = 128
BLK = 64


def shards(query_rows, key_rows, value_rows, output_grad, out_weight, clusters):
    rows_here = query_rows.shape[0]
    columns = query_rows.shape[1]
    heads_here = columns // HS
    score_scale = HS ** (-0.5)
    all_rows = rows_here * lax.axis_size("seq")
    block_count = clusters.shape[0]
    local_blocks = rows_here // BLK
    tile_blocks = min(max(512 // BLK, 1), block_count)
    tile_rows = tile_blocks * BLK
    full_grad = lax.all_gather(output_grad, "head", axis=1, tiled=True)
    grad_attended = jnp.dot(full_grad, out_weight, preferred_element_type=jnp.float32).astype(
        jnp.bfloat16
    )
    keys_all, values_all = (
        lax.all_gather(key_rows, "seq", axis=0, tiled=True),
        lax.all_gather(value_rows, "seq", axis=0, tiled=True),
    )
    query_split = query_rows.reshape(rows_here, heads_here, HS)
    grad_split = grad_attended.reshape(rows_here, heads_here, HS)
    key_blocks = keys_all.reshape(block_count, BLK, columns)
    value_blocks = values_all.reshape(block_count, BLK, columns)
    block_ids = jnp.arange(block_count, dtype=jnp.int32)
    first_block = lax.axis_index("seq") * local_blocks

    def block_list(local):
        query_block = first_block + local
        usable = (clusters == clusters[query_block]) & (block_ids <= query_block)
        order = jnp.argsort(jnp.where(usable, block_ids, block_count + block_ids))
        padded = jnp.concatenate([order, jnp.zeros((tile_blocks,), jnp.int32)])
        return (padded, jnp.sum(usable.astype(jnp.int32)), query_block)

    lists, counts, query_blocks = jax.vmap(block_list)(jnp.arange(local_blocks, dtype=jnp.int32))

    def tile_data(local, turn):
        picked = lax.dynamic_slice_in_dim(lists[local], turn * tile_blocks, tile_blocks, 0)
        tile_keys = key_blocks[picked].reshape(tile_rows, heads_here, HS)
        tile_values = value_blocks[picked].reshape(tile_rows, heads_here, HS)
        slot_ok = turn * tile_blocks + jnp.arange(tile_blocks, dtype=jnp.int32) < counts[local]
        key_pos = (picked[:, None] * BLK + jnp.arange(BLK, dtype=jnp.int32)[None, :]).reshape(
            tile_rows
        )
        query_pos = query_blocks[local] * BLK + jnp.arange(BLK, dtype=jnp.int32)
        permitted = jnp.repeat(slot_ok, BLK)[None, :] & (key_pos[None, :] <= query_pos[:, None])
        return (picked, tile_keys, tile_values, permitted)

    def tile_scores(query_block, tile_keys, permitted):
        scores = (
            jnp.einsum("qhd,khd->hqk", query_block, tile_keys, preferred_element_type=jnp.float32)
            * score_scale
        )
        return jnp.where(permitted[None], scores, -jnp.inf)

    def one_block(local, state):
        query_out, log_out, corr_out, key_buffer, value_buffer = state
        query_block = lax.dynamic_slice_in_dim(query_split, local * BLK, BLK, 0)
        grad_block = lax.dynamic_slice_in_dim(grad_split, local * BLK, BLK, 0)
        turns = (counts[local] + tile_blocks - 1) // tile_blocks

        def first_pass(turn, carry):
            running_max, running_total = carry
            picked, tile_keys, tile_values, permitted = tile_data(local, turn)
            scores = tile_scores(query_block, tile_keys, permitted)
            new_max = jnp.maximum(running_max, jnp.max(scores, axis=2))
            running_total = running_total * jnp.exp(running_max - new_max) + jnp.sum(
                jnp.exp(scores - new_max[:, :, None]), axis=2
            )
            return (new_max, running_total)

        start_max = jnp.full((heads_here, BLK), -jnp.inf, jnp.float32)
        start_total = jnp.zeros((heads_here, BLK), jnp.float32)
        row_max, row_total = lax.fori_loop(0, turns, first_pass, (start_max, start_total))
        log_total = row_max + jnp.log(row_total)

        def second_pass(turn, running):
            picked, tile_keys, tile_values, permitted = tile_data(local, turn)
            scores = tile_scores(query_block, tile_keys, permitted)
            probability_b = jnp.exp(scores - log_total[:, :, None]).astype(jnp.bfloat16)
            return running + jnp.einsum(
                "hqk,khd->qhd", probability_b, tile_values, preferred_element_type=jnp.float32
            )

        attended = lax.fori_loop(
            0, turns, second_pass, jnp.zeros((BLK, heads_here, HS), jnp.float32)
        ).astype(jnp.bfloat16)
        correction = jnp.sum(grad_block.astype(jnp.float32) * attended.astype(jnp.float32), axis=2)

        def third_pass(turn, carry):
            query_acc, key_acc, value_acc = carry
            picked, tile_keys, tile_values, permitted = tile_data(local, turn)
            scores = tile_scores(query_block, tile_keys, permitted)
            probability = jnp.exp(scores - log_total[:, :, None])
            grad_prob = jnp.einsum(
                "qhd,khd->hqk", grad_block, tile_values, preferred_element_type=jnp.float32
            )
            grad_score = (
                probability * (grad_prob - correction.T[:, :, None]) * score_scale
            ).astype(jnp.bfloat16)
            query_acc = query_acc + jnp.einsum(
                "hqk,khd->qhd", grad_score, tile_keys, preferred_element_type=jnp.float32
            )
            key_term = jnp.einsum(
                "hqk,qhd->khd", grad_score, query_block, preferred_element_type=jnp.float32
            )
            value_term = jnp.einsum(
                "hqk,qhd->khd",
                probability.astype(jnp.bfloat16),
                grad_block,
                preferred_element_type=jnp.float32,
            )
            key_acc = key_acc.at[picked].add(key_term.reshape(tile_blocks, BLK, columns))
            value_acc = value_acc.at[picked].add(value_term.reshape(tile_blocks, BLK, columns))
            return (query_acc, key_acc, value_acc)

        query_acc, key_buffer, value_buffer = lax.fori_loop(
            0,
            turns,
            third_pass,
            (jnp.zeros((BLK, heads_here, HS), jnp.float32), key_buffer, value_buffer),
        )
        query_out = lax.dynamic_update_slice_in_dim(
            query_out, query_acc.reshape(BLK, columns).astype(jnp.bfloat16), local * BLK, 0
        )
        log_out = lax.dynamic_update_slice_in_dim(log_out, log_total.T, local * BLK, 0)
        corr_out = lax.dynamic_update_slice_in_dim(corr_out, correction, local * BLK, 0)
        return (query_out, log_out, corr_out, key_buffer, value_buffer)

    start = (
        jnp.zeros((rows_here, columns), jnp.bfloat16),
        jnp.zeros((rows_here, heads_here), jnp.float32),
        jnp.zeros((rows_here, heads_here), jnp.float32),
        jnp.zeros((block_count, BLK, columns), jnp.float32),
        jnp.zeros((block_count, BLK, columns), jnp.float32),
    )
    query_grad, log_rows, correction, key_buffer, value_buffer = lax.fori_loop(
        0, local_blocks, one_block, start
    )
    joined = jnp.concatenate(
        [key_buffer.reshape(all_rows, columns), value_buffer.reshape(all_rows, columns)], axis=1
    )
    summed = lax.psum_scatter(
        joined.astype(jnp.bfloat16), "seq", scatter_dimension=0, tiled=True
    ).astype(jnp.float32)
    key_grad = summed[:, :columns].astype(jnp.bfloat16)
    value_grad = summed[:, columns:].astype(jnp.bfloat16)
    return (query_grad, key_grad, value_grad)


def solution(mesh):
    return jax.shard_map(
        shards,
        mesh=mesh,
        in_specs=(
            P("seq", "head"),
            P("seq", "head"),
            P("seq", "head"),
            P("seq", "head"),
            P(None, "head"),
            P(),
        ),
        out_specs=(P("seq", "head"), P("seq", "head"), P("seq", "head")),
        check_vma=False,
    )
```

profile of v0, /device:TPU:2, one launch (start us, length us, event | category | flops | bytes accessed | tf_op | source)
XLA Modules:
  0.0 414.0 jit_solution(17297681794545578149)
XLA Ops:
  13.8 38.3 %all-gather.6.cloned.1.call-done = bf16[128,5120]{1,0:T(8,128)(2,1)} async-done(((bf16[128,640]{1,0:T(8,128)(2,1)}), bf16[128,5120]{1,0:T(8,128)(2,1)}) %all-gather.6.cloned.1.call-update) | async-done | bytes 1310736 | tf_op jit(solution)/shard_map/all_gather | solution.py:20
  52.1 3.4 convolution_convert_fusion
  55.7 46.5 %all-gather.4.cloned.1.call-done = bf16[4096,384]{1,0:T(8,128)(2,1)} async-done(((bf16[128,384]{1,0:T(8,128)(2,1)}), bf16[4096,384]{1,0:T(8,128)(2,1)}) %all-gather.4.cloned.1.call-update) | async-done | bytes 3145744 | tf_op jit(solution)/shard_map/all_gather | solution.py:25
  102.3 51.9 %all-gather.8.cloned.1.call-done = bf16[4096,384]{1,0:T(8,128)(2,1)} async-done(((bf16[128,384]{1,0:T(8,128)(2,1)}), bf16[4096,384]{1,0:T(8,128)(2,1)}) %all-gather.8.cloned.1.call-update) | async-done | bytes 3145744 | tf_op jit(solution)/shard_map/all_gather | solution.py:26
  154.1 3.4 broadcast.357.clone
  157.6 3.4 broadcast.357
  161.0 60.6 %while.160 = (s32[]{:T(128)}, bf16[128,384]{1,0:T(8,128)(2,1)S(1)}, f32[64,64,384]{2,1,0:T(8,128)}, f32[64,64,384]{2,1,0:T(8,128)}, s32[2]{0:T(128)S(1)}, /*inde...) while((s32[]{:T(128)}, bf16[128,384]{1,0:T(8,128)(2,1)S(1)}, ...), condition=%wide.region_14.15_spmd, body=%wide.region_2.14_spmd.sunk | while | flops 203789568 | bytes 27048524 | solution.py:144
  163.6 4.5 %while.161 = (s32[]{:T(128)}, f32[3,64]{1,0:T(4,128)S(1)}, f32[3,64]{1,0:T(4,128)S(1)}, s32[]{:T(128)}, s32[1]{0:T(128)}, /*index=5*/s32[2,72]{1,0:T(2,128)S(1)}...) while((s32[]{:T(128)}, f32[3,64]{1,0:T(4,128)S(1)}, ...), condition=%wide.region_6.6_spmd, body=%wide.region_3.5_spmd.sunk | while | flops 25724920 | bytes 2892503 | solution.py:81
  164.8 2.5 gather_fusion
  168.1 7.0 %while.162 = (s32[]{:T(128)}, f32[64,3,128]{2,0,1:T(8,128)S(1)}, s32[]{:T(128)}, s32[2,72]{1,0:T(2,128)S(1)}, s32[]{:T(128)}, /*index=5*/bf16[64,64,384]{2,1,0:T...) while((s32[]{:T(128)}, f32[64,3,128]{2,0,1:T(8,128)S(1)}, ...), condition=%wide.region_8.8_spmd, body=%wide.region_7.7_spmd.sunk | while | flops 50816632 | bytes 4259583 | solution.py:92
  169.4 2.5 gather_fusion.2
  172.1 2.5 gather_fusion.1
  175.3 16.0 %while.163 = (s32[]{:T(128)}, f32[64,3,128]{2,0,1:T(8,128)S(1)}, f32[64,64,384]{2,1,0:T(8,128)}, f32[64,64,384]{2,1,0:T(8,128)}, s32[]{:T(128)}, /*index=5*/s32[...) while((s32[]{:T(128)}, f32[64,3,128]{2,0,1:T(8,128)S(1)}, ...), condition=%wide.region_13.13_spmd, body=%wide.region_10.12_spmd.sunk | while | flops 127100536 | bytes 19153504 | solution.py:124
  176.5 2.5 gather_fusion.4
  185.2 3.0 scatter_fusion
  188.2 3.1 scatter_fusion.1
  193.9 4.5 %while.161 = (s32[]{:T(128)}, f32[3,64]{1,0:T(4,128)S(1)}, f32[3,64]{1,0:T(4,128)S(1)}, s32[]{:T(128)}, s32[1]{0:T(128)}, /*index=5*/s32[2,72]{1,0:T(2,128)S(1)}...) while((s32[]{:T(128)}, f32[3,64]{1,0:T(4,128)S(1)}, ...), condition=%wide.region_6.6_spmd, body=%wide.region_3.5_spmd.sunk | while | flops 25724920 | bytes 2892503 | solution.py:81
  198.5 7.0 %while.162 = (s32[]{:T(128)}, f32[64,3,128]{2,0,1:T(8,128)S(1)}, s32[]{:T(128)}, s32[2,72]{1,0:T(2,128)S(1)}, s32[]{:T(128)}, /*index=5*/bf16[64,64,384]{2,1,0:T...) while((s32[]{:T(128)}, f32[64,3,128]{2,0,1:T(8,128)S(1)}, ...), condition=%wide.region_8.8_spmd, body=%wide.region_7.7_spmd.sunk | while | flops 50816632 | bytes 4259583 | solution.py:92
  205.6 16.0 %while.163 = (s32[]{:T(128)}, f32[64,3,128]{2,0,1:T(8,128)S(1)}, f32[64,64,384]{2,1,0:T(8,128)}, f32[64,64,384]{2,1,0:T(8,128)}, s32[]{:T(128)}, /*index=5*/s32[...) while((s32[]{:T(128)}, f32[64,3,128]{2,0,1:T(8,128)S(1)}, ...), condition=%wide.region_13.13_spmd, body=%wide.region_10.12_spmd.sunk | while | flops 127100536 | bytes 19153504 | solution.py:124
  215.5 3.1 scatter_fusion
  218.5 3.1 scatter_fusion.1
  221.6 3.5 convert.11
  226.8 3.2 pad_maximum_fusion
  230.0 175.9 %reduce-scatter.2.cloned.1.call-done = bf16[128,768]{1,0:T(8,128)(2,1)} async-done(((bf16[4096,768]{1,0:T(8,128)(2,1)}), bf16[128,768]{1,0:T(8,128)(2,1)}) %reduce-scatter.2.cloned.1.call-update) | async-done | bytes 196624 | tf_op jit(solution)/shard_map/reduce_scatter | solution.py:150
  (157 shorter events, 45.1 us)
Async XLA Ops:
  7.2 44.9 %all-gather.6.cloned.1.call-start = ((), (), s32[]{:S(2)}) async-start(), calls=%async_computation.2 | async-start | bytes 1474560 | tf_op jit(solution)/shard_map/all_gather | solution.py:20
  7.9 94.4 %all-gather.4.cloned.1.call-start = ((), (), s32[]{:S(2)}) async-start(), calls=%async_computation.1 | async-start | bytes 3244032 | tf_op jit(solution)/shard_map/all_gather | solution.py:25
  8.6 145.5 %all-gather.8.cloned.1.call-start = ((), (), s32[]{:S(2)}) async-start(), calls=%async_computation.3 | async-start | bytes 3244032 | tf_op jit(solution)/shard_map/all_gather | solution.py:26
  9.4 396.5 %reduce-scatter.2.cloned.1.call-start = ((), (), s32[]{:S(2)}) async-start(), calls=%async_computation.4 | async-start | bytes 6488064 | tf_op jit(solution)/shard_map/reduce_scatter | solution.py:150
  221.6 5.2 %copy-start.1 = (bf16[128,384]{1,0:T(8,128)(2,1)}, bf16[128,384]{1,0:T(8,128)(2,1)S(1)}, u32[]{:S(2)}) copy-start(bf16[128,384]{1,0:T(8,128)(2,1)S(1)} %get-tuple-element.874) | copy-start | bytes 294916
  221.6 4.6 %copy-start = (f32[64,64,384]{2,1,0:T(8,128)S(1)}, f32[64,64,384]{2,1,0:T(8,128)}, u32[]{:S(2)}) copy-start(f32[64,64,384]{2,1,0:T(8,128)} %get-tuple-element.879) | copy-start | bytes 18874372
Sparse Core Ops, SparseCore 0:
  9.8 42.2 all-gather.5
  54.6 47.5 all-gather.3
  104.8 49.2 all-gather.7
  230.1 175.6 reduce-scatter.1
where the time goes:
time: 416 us; the launch traced here: 414 us
  waiting for transfers between devices  315 us (76%)
  local copies, waits for them, and re-layouts  46.6 us (11%)
  other arithmetic  27.7 us (7%)
  between operations  13.9 us (3%)
  matrix products  7.66 us (2%)
    reduce_scatter x1, waiting for transfers between devices, shards(): lax.psum_scatter(joined.astype(jnp.bfloat16), 'seq', scatter_dimension=0,...  176 us
    all_gather x1, waiting for transfers between devices, shards(): lax.all_gather(value_rows, 'seq', axis=0, tiled=True)  51.9 us
    all_gather x1, waiting for transfers between devices, shards(): lax.all_gather(key_rows, 'seq', axis=0, tiled=True)  46.5 us
    all_gather x1, waiting for transfers between devices, shards(): full_grad = lax.all_gather(output_grad, 'head', axis=1, tiled=True)  38.3 us
    gather x6, local copies, waits for them, and re-layouts, tile_data(): tile_keys = key_blocks[picked].reshape(tile_rows, heads_here, HS)  15.1 us
    gather x4, local copies, waits for them, and re-layouts, tile_data(): tile_values = value_blocks[picked].reshape(tile_rows, heads_here, HS)  10.1 us
  transfers between devices with their start and end apart: 4, of which 4 were waited for; matrix products, arithmetic and copies ran while one was open for 2% of the time, Pallas kernels for 0%

commit v1 on v0

--- a/solution.py
+++ b/solution.py
@@ -21,8 +21,17 @@
     grad_attended = jnp.dot(full_grad, out_weight, preferred_element_type=jnp.float32).astype(
         jnp.bfloat16
     )
+    choose_sources_all = lambda page, axis_tag: jnp.concatenate(
+        lax.all_to_all(
+            jnp.stack([page] * lax.axis_size(axis_tag), axis=0),
+            axis_tag,
+            split_axis=0,
+            concat_axis=0,
+        ),
+        axis=0,
+    )
     keys_all, values_all = (
-        lax.all_gather(key_rows, "seq", axis=0, tiled=True),
+        choose_sources_all(key_rows, "seq"),
         lax.all_gather(value_rows, "seq", axis=0, tiled=True),
     )
     query_split = query_rows.reshape(rows_here, heads_here, HS)

time: 416 us -> 364 us (0.88)
  waiting for transfers between devices: 315 us -> 254 us
  starting transfers between devices: 0.15 us -> 7.79 us
    all_gather x1 -> x0, waiting for transfers between devices: 46.5 us -> none  [shards(): lax.all_gather(key_rows, 'seq', axis=0, tiled=True)]
    all_gather x1, waiting for transfers between devices: 38.3 us -> 30.3 us  [shards(): full_grad = lax.all_gather(output_grad, 'head', axis=1, tiled=True)]
    all_to_all x0 -> x1, starting transfers between devices: none -> 7.67 us  [shards(): lax.all_to_all(jnp.stack([page] * lax.axis_size(axis_tag), axis=0), axis_...]
    all_gather x1, waiting for transfers between devices: 51.9 us -> 45.7 us  [shards(): lax.all_gather(value_rows, 'seq', axis=0, tiled=True)]
    another operation x10 -> x11, local copies, waits for them, and re-layouts: 6.91 us -> 9.94 us
where the time goes in v1:
time: 364 us; the launch traced here: 362 us
  waiting for transfers between devices  254 us (70%)
  local copies, waits for them, and re-layouts  48.1 us (13%)
  other arithmetic  27.1 us (7%)
  between operations  13.9 us (4%)
  starting transfers between devices  7.79 us (2%)
  matrix products  7.66 us (2%)
    reduce_scatter x1, waiting for transfers between devices, shards(): lax.psum_scatter(joined.astype(jnp.bfloat16), 'seq', scatter_dimension=0,...  176 us
    all_gather x1, waiting for transfers between devices, shards(): lax.all_gather(value_rows, 'seq', axis=0, tiled=True)  45.7 us
    all_gather x1, waiting for transfers between devices, shards(): full_grad = lax.all_gather(output_grad, 'head', axis=1, tiled=True)  30.3 us
    gather x6, local copies, waits for them, and re-layouts, tile_data(): tile_keys = key_blocks[picked].reshape(tile_rows, heads_here, HS)  15.1 us
    gather x4, local copies, waits for them, and re-layouts, tile_data(): tile_values = value_blocks[picked].reshape(tile_rows, heads_here, HS)  10.1 us
    all_to_all x1, starting transfers between devices, shards(): lax.all_to_all(jnp.stack([page] * lax.axis_size(axis_tag), axis=0), axis_...  7.67 us
  transfers between devices with their start and end apart: 4, of which 4 were waited for; matrix products, arithmetic and copies ran while one was open for 2% of the time, Pallas kernels for 0%

profile of v1, /device:TPU:2, one launch (start us, length us, event | category | flops | bytes accessed | tf_op | source)
XLA Modules:
  0.0 362.1 jit_solution(5494485694600730337)
XLA Ops:
  8.7 3.0 stack.2
  11.7 7.7 %all-to-all-start = ((bf16[32,128,384]{2,1,0:T(8,128)(2,1)}), bf16[32,128,384]{2,1,0:T(8,128)(2,1)}, u32[]{:S(2)}, u32[]{:S(2)}) async-start(bf16[32,128,384]{2,1,0:T(8,128)(2,1)} %stack.2), calls=%async_computation | async-start | bytes 6291456 | tf_op jit(solution)/shard_map/all_to_all | solution.py:25
  21.6 30.3 %all-gather.3.cloned.1.call-done = bf16[128,5120]{1,0:T(8,128)(2,1)} async-done(((bf16[128,640]{1,0:T(8,128)(2,1)}), bf16[128,5120]{1,0:T(8,128)(2,1)}) %all-gather.3.cloned.1.call-update) | async-done | bytes 1310736 | tf_op jit(solution)/shard_map/all_gather | solution.py:20
  51.9 3.4 convolution_convert_fusion
  56.5 45.7 %all-gather.5.cloned.1.call-done = bf16[4096,384]{1,0:T(8,128)(2,1)} async-done(((bf16[128,384]{1,0:T(8,128)(2,1)}), bf16[4096,384]{1,0:T(8,128)(2,1)}) %all-gather.5.cloned.1.call-update) | async-done | bytes 3145744 | tf_op jit(solution)/shard_map/all_gather | solution.py:35
  102.2 3.4 broadcast.359.clone
  105.6 3.4 broadcast.359
  109.0 60.6 %while.160 = (s32[]{:T(128)}, bf16[128,384]{1,0:T(8,128)(2,1)S(1)}, f32[64,64,384]{2,1,0:T(8,128)}, f32[64,64,384]{2,1,0:T(8,128)}, s32[2]{0:T(128)S(1)}, /*inde...) while((s32[]{:T(128)}, bf16[128,384]{1,0:T(8,128)(2,1)S(1)}, ...), condition=%wide.region_14.15_spmd, body=%wide.region_2.14_spmd.sunk | while | flops 203789568 | bytes 27048524 | solution.py:153
  111.6 4.5 %while.161 = (s32[]{:T(128)}, f32[3,64]{1,0:T(4,128)S(1)}, f32[3,64]{1,0:T(4,128)S(1)}, s32[]{:T(128)}, s32[1]{0:T(128)}, /*index=5*/s32[2,72]{1,0:T(2,128)S(1)}...) while((s32[]{:T(128)}, f32[3,64]{1,0:T(4,128)S(1)}, ...), condition=%wide.region_6.6_spmd, body=%wide.region_3.5_spmd.sunk | while | flops 25724920 | bytes 2892503 | solution.py:90
  112.9 2.5 gather_fusion
  116.2 7.0 %while.162 = (s32[]{:T(128)}, f32[64,3,128]{2,0,1:T(8,128)S(1)}, s32[]{:T(128)}, s32[2,72]{1,0:T(2,128)S(1)}, s32[]{:T(128)}, /*index=5*/bf16[64,64,384]{2,1,0:T...) while((s32[]{:T(128)}, f32[64,3,128]{2,0,1:T(8,128)S(1)}, ...), condition=%wide.region_8.8_spmd, body=%wide.region_7.7_spmd.sunk | while | flops 50816632 | bytes 4259583 | solution.py:101
  117.4 2.5 gather_fusion.2
  120.1 2.5 gather_fusion.1
  123.3 16.0 %while.163 = (s32[]{:T(128)}, f32[64,3,128]{2,0,1:T(8,128)S(1)}, f32[64,64,384]{2,1,0:T(8,128)}, f32[64,64,384]{2,1,0:T(8,128)}, s32[]{:T(128)}, /*index=5*/s32[...) while((s32[]{:T(128)}, f32[64,3,128]{2,0,1:T(8,128)S(1)}, ...), condition=%wide.region_13.13_spmd, body=%wide.region_10.12_spmd.sunk | while | flops 127100536 | bytes 19153504 | solution.py:133
  133.2 3.0 scatter_fusion
  136.2 3.1 scatter_fusion.1
  141.9 4.5 %while.161 = (s32[]{:T(128)}, f32[3,64]{1,0:T(4,128)S(1)}, f32[3,64]{1,0:T(4,128)S(1)}, s32[]{:T(128)}, s32[1]{0:T(128)}, /*index=5*/s32[2,72]{1,0:T(2,128)S(1)}...) while((s32[]{:T(128)}, f32[3,64]{1,0:T(4,128)S(1)}, ...), condition=%wide.region_6.6_spmd, body=%wide.region_3.5_spmd.sunk | while | flops 25724920 | bytes 2892503 | solution.py:90
  146.5 7.0 %while.162 = (s32[]{:T(128)}, f32[64,3,128]{2,0,1:T(8,128)S(1)}, s32[]{:T(128)}, s32[2,72]{1,0:T(2,128)S(1)}, s32[]{:T(128)}, /*index=5*/bf16[64,64,384]{2,1,0:T...) while((s32[]{:T(128)}, f32[64,3,128]{2,0,1:T(8,128)S(1)}, ...), condition=%wide.region_8.8_spmd, body=%wide.region_7.7_spmd.sunk | while | flops 50816632 | bytes 4259583 | solution.py:101
  153.6 16.0 %while.163 = (s32[]{:T(128)}, f32[64,3,128]{2,0,1:T(8,128)S(1)}, f32[64,64,384]{2,1,0:T(8,128)}, f32[64,64,384]{2,1,0:T(8,128)}, s32[]{:T(128)}, /*index=5*/s32[...) while((s32[]{:T(128)}, f32[64,3,128]{2,0,1:T(8,128)S(1)}, ...), condition=%wide.region_13.13_spmd, body=%wide.region_10.12_spmd.sunk | while | flops 127100536 | bytes 19153504 | solution.py:133
  163.5 3.1 scatter_fusion
  166.6 3.1 scatter_fusion.1
  169.7 3.5 convert.11
  174.8 3.2 pad_maximum_fusion
  178.0 175.9 %reduce-scatter.2.cloned.1.call-done = bf16[128,768]{1,0:T(8,128)(2,1)} async-done(((bf16[4096,768]{1,0:T(8,128)(2,1)}), bf16[128,768]{1,0:T(8,128)(2,1)}) %reduce-scatter.2.cloned.1.call-update) | async-done | bytes 196624 | tf_op jit(solution)/shard_map/reduce_scatter | solution.py:159
  (161 shorter events, 45.7 us)
Async XLA Ops:
  7.2 12.3 %copy-start = (s32[64]{0:T(128)S(1)}, s32[64]{0:T(128)}, u32[]{:S(2)}) copy-start(s32[64]{0:T(128)} %param.19) | copy-start | bytes 772
  7.2 14.2 %copy-start.2 = (bf16[128,384]{1,0:T(8,128)(2,1)S(1)}, bf16[128,384]{1,0:T(8,128)(2,1)}, u32[]{:S(2)}) copy-start(bf16[128,384]{1,0:T(8,128)(2,1)} %param.14) | copy-start | bytes 294916
  7.2 44.7 %all-gather.3.cloned.1.call-start = ((), (), s32[]{:S(2)}) async-start(), calls=%async_computation.2 | async-start | bytes 1474560 | tf_op jit(solution)/shard_map/all_gather | solution.py:20
  7.9 94.2 %all-gather.5.cloned.1.call-start = ((), (), s32[]{:S(2)}) async-start(), calls=%async_computation.3 | async-start | bytes 3244032 | tf_op jit(solution)/shard_map/all_gather | solution.py:35
  11.7 44.8 %all-to-all-start = ((bf16[32,128,384]{2,1,0:T(8,128)(2,1)}), bf16[32,128,384]{2,1,0:T(8,128)(2,1)}, u32[]{:S(2)}, u32[]{:S(2)}) async-start(bf16[32,128,384]{2,1,0:T(8,128)(2,1)} %stack.2), calls=%async_computation | async-start | bytes 6291456 | tf_op jit(solution)/shard_map/all_to_all | solution.py:25
  19.4 334.6 %reduce-scatter.2.cloned.1.call-start = ((), (), s32[]{:S(2)}) async-start(), calls=%async_computation.4 | async-start | bytes 6488064 | tf_op jit(solution)/shard_map/reduce_scatter | solution.py:159
  169.7 5.2 %copy-start.3 = (bf16[128,384]{1,0:T(8,128)(2,1)}, bf16[128,384]{1,0:T(8,128)(2,1)S(1)}, u32[]{:S(2)}) copy-start(bf16[128,384]{1,0:T(8,128)(2,1)S(1)} %get-tuple-element.874) | copy-start | bytes 294916
  169.7 4.6 %copy-start.1 = (f32[64,64,384]{2,1,0:T(8,128)S(1)}, f32[64,64,384]{2,1,0:T(8,128)}, u32[]{:S(2)}) copy-start(f32[64,64,384]{2,1,0:T(8,128)} %get-tuple-element.879) | copy-start | bytes 18874372
Sparse Core Ops, SparseCore 0:
  9.8 42.0 all-gather.2
  54.4 47.6 all-gather.4
  178.1 175.7 reduce-scatter.1
